TPU v7x, 32 devices: a whole 2x2x4 slice. The times are simulated.
32 devices in a mesh: ray: 16 (over z, x, core), vox: 2 (over y).
Axes of the slice: x: 2, y: 2, z: 4, core: 2. Of those that a mesh axis runs over, the one named last changes fastest.
Arguments:
- tiles: bfloat16 [16, 2, 32, 128, 128], P('ray', 'vox'), may hold values from -0.1875 to 0.1875
- tile_scale: float32 [16, 2, 32], P('ray', 'vox'), may hold values from 0.25 to 4
- tile_row: int32 [16, 2, 32], P('ray', 'vox'), may hold values from 0 to 7
- tile_col: int32 [16, 2, 32], P('ray', 'vox'), may hold values from 0 to 1023
- tile_count: int32 [16, 2], P('ray', 'vox'), may hold values from 16 to 32, as said below
- delays: float32 [16384], P('ray'), may hold values from -6 to 6
- ray_receiver: int32 [16384], P('ray'), may hold values from 0 to 95
- receiver_weight: float32 [1536], P('ray'), may hold values from 0.5 to 2
- smooth_scale: float32 [64], replicated, may hold values from 0.05 to 0.5
Outputs:
- density: float32 [64, 2, 16, 128], P('ray', None, 'vox')
- rays_vec: float32 [16384], P('ray')
Inputs may be any that keep to these rules, and one draw needn't show every extreme that they name: `tile_count`: each ray group and voxel slab has between 16 and 32 live tile slots, and some has all 32 in every draw.
All inputs are finite; a program needn't handle non-finite values.
Results may differ from a plain program's by a relative error of at most 0.013.
Values sent between devices are 32-bit elements; how exact they have to be, the bound alone decides.
No kernel may reach another device: no remote copies, remote signals or barrier semaphores. Data moves between devices by JAX's collectives and lax.ppermute only.
A program may use at most 64 MiB of HBM per device.

v0:
```python
import jax
import jax.numpy as jnp
from jax import lax
from jax.sharding import PartitionSpec as P

ALT = 64
EPOCHS = 2
LAT = 128
LON_DEV = 8
RAY_TILE = 128
RT = 8
ITERS = 2
LATERAL = 1.0
VERTICAL = 4.0
TEMPORAL = 0.5


def with_halo(block, sides, width):
    for axis, dim in sides:
        count = lax.axis_size(axis)
        forward = [(i, i + 1) for i in range(count - 1)]
        backward = [(target, source) for source, target in forward]
        low = lax.ppermute(
            lax.slice_in_dim(block, block.shape[dim] - width, None, axis=dim), axis, forward
        )
        high = lax.ppermute(lax.slice_in_dim(block, 0, width, axis=dim), axis, backward)
        block = jnp.concatenate([low, block, high], axis=dim)
    return block


def stencil(padded, field):
    lateral = padded[1:-1, 1:-1, 2:, 1:-1] + padded[1:-1, 1:-1, :-2, 1:-1]
    lateral = lateral + padded[1:-1, 1:-1, 1:-1, 2:] + padded[1:-1, 1:-1, 1:-1, :-2]
    vertical = padded[2:, 1:-1, 1:-1, 1:-1] + padded[:-2, 1:-1, 1:-1, 1:-1]
    temporal = padded[1:-1, 2:, 1:-1, 1:-1] + padded[1:-1, :-2, 1:-1, 1:-1]
    centre = 2.0 * (2.0 * LATERAL + VERTICAL + TEMPORAL)
    return centre * field - LATERAL * lateral - VERTICAL * vertical - TEMPORAL * temporal


def laplace_local(field):
    padded = with_halo(field, (("vox", 2),), 1)
    padded = jnp.pad(padded, ((1, 1), (1, 1), (0, 0), (1, 1)))
    return stencil(padded, field)


def on_device(
    tiles,
    tile_scale,
    tile_row,
    tile_col,
    tile_count,
    delays,
    ray_receiver,
    receiver_weight,
    smooth_scale,
):
    block = tiles[0, 0]
    row_index = tile_row[0, 0]
    col_index = tile_col[0, 0]
    slots = block.shape[0]
    live = (jnp.arange(slots) < tile_count[0, 0]).astype(jnp.float32)
    effective = tile_scale[0, 0] * live
    table_size = receiver_weight.shape[0]
    matches = ray_receiver[:, None] == jnp.arange(table_size)[None, :]
    ray_weight = jnp.sum(jnp.where(matches, receiver_weight[None, :], 0.0), axis=1)
    damping = smooth_scale[:, None, None, None]
    lines_total = ALT * EPOCHS * LON_DEV
    share_rows = ALT // lax.axis_size("ray")
    offset = lax.axis_index("ray") * share_rows
    ray_onehot = (row_index[None, :] == jnp.arange(RT)[:, None]).astype(jnp.float32)

    def ray_total(values):
        return lax.psum(jnp.sum(values * values), "ray")

    def slab_total(values):
        return lax.psum(jnp.sum(values * values), "vox")

    def adjoint_lines(weighted):
        picked = jnp.take(weighted.reshape(RT, RAY_TILE), row_index, axis=0)
        return (
            jnp.einsum("ktl,kt->kl", block, picked, preferred_element_type=jnp.float32)
            * effective[:, None]
        )

    def pull_back(weighted):
        contrib = adjoint_lines(weighted)
        onehot = (col_index[None, :] == jnp.arange(lines_total)[:, None]).astype(jnp.float32)
        summed = jnp.dot(onehot, contrib, precision=lax.Precision.HIGHEST).reshape(
            ALT, EPOCHS, LON_DEV, LAT
        )
        return lax.psum(summed, "ray")

    def right_norm_of(values):
        return jnp.sqrt(slab_total(values))

    rays_vec = ray_weight * delays
    left_norm = jnp.sqrt(ray_total(rays_vec))
    rays_vec = rays_vec / left_norm
    smooth_vec = jnp.zeros((ALT, EPOCHS, LON_DEV, LAT), jnp.float32)
    right = pull_back((ray_weight * rays_vec).astype(jnp.bfloat16))
    right_norm = right_norm_of(right)
    right = right / right_norm
    search = right
    density = jnp.zeros_like(right)
    resid_bar = left_norm
    diag_bar = right_norm
    for iteration in range(ITERS):
        current = right
        smooth_vec = damping * laplace_local(current) - right_norm * smooth_vec
        lines = current.reshape(lines_total, LAT).astype(jnp.bfloat16)
        forward_picked = jnp.take(lines, col_index, axis=0)
        rays = (
            jnp.einsum("ktl,kl->kt", block, forward_picked, preferred_element_type=jnp.float32)
            * effective[:, None]
        )
        partial_value = jnp.dot(ray_onehot, rays, precision=lax.Precision.HIGHEST).reshape(-1)
        ray_sums = lax.psum(partial_value, "vox")
        smooth_sq = slab_total(smooth_vec)
        rays_vec = ray_weight * ray_sums - right_norm * rays_vec
        left_norm = jnp.sqrt(ray_total(rays_vec) + smooth_sq)
        rays_vec = rays_vec / left_norm
        smooth_vec = smooth_vec / left_norm
        smoothing = laplace_local(damping * smooth_vec)
        right = (
            pull_back((ray_weight * rays_vec).astype(jnp.bfloat16)) + smoothing - left_norm * right
        )
        right_norm = right_norm_of(right)
        right = right / right_norm
        diag_new = jnp.sqrt(diag_bar * diag_bar + left_norm * left_norm)
        cosine = diag_bar / diag_new
        sine_value = left_norm / diag_new
        coupling = sine_value * right_norm
        diag_bar = -cosine * right_norm
        step_size = cosine * resid_bar
        resid_bar = sine_value * resid_bar
        density = density + step_size / diag_new * search
        search = right - coupling / diag_new * search
    density_out = lax.dynamic_slice_in_dim(density, offset, share_rows, 0)
    return (density_out, rays_vec)


def solution(mesh):
    in_specs = (
        P("ray", "vox", None, None, None),
        P("ray", "vox", None),
        P("ray", "vox", None),
        P("ray", "vox", None),
        P("ray", "vox"),
        P("ray"),
        P("ray"),
        P("ray"),
        P(),
    )
    out_specs = (P("ray", None, "vox", None), P("ray"))
    return jax.shard_map(
        on_device, mesh=mesh, in_specs=in_specs, out_specs=out_specs, check_vma=False
    )
```

profile of v0, /device:TPU:0, one launch (start us, length us, event | category | flops | bytes accessed | tf_op | source)
XLA Modules:
  0.0 363.2 jit_solution(5082143402132900104)
XLA Ops:
  7.2 0.0 copy-start
  7.2 0.0 copy-start.3
  7.2 0.0 all-reduce.8.cloned.1.call-start
  7.2 0.7 compare_select_fusion.1
  8.0 0.7 compare_and_fusion.1
  8.6 0.8 select_reduce_fusion
  9.5 1.3 multiply_reduce_fusion.5
  10.8 35.5 %psum.77 = f32[]{:T(128)} all-reduce(f32[]{:T(128)} %get-tuple-element.20), channel_id=1, replica_groups=mesh['ray'=16,'vox'=2] {'ray'}, use_global_device_ids=true, to_apply=%region_2.3 | all-reduce | flops 1 | bytes 8 | tf_op jit(solution)/shard_map/psum | solution.py:73
  47.6 0.6 gather_fusion
  48.2 0.1 select_bitcast_fusion.3
  48.3 0.4 fusion.11
  48.7 0.7 compare_select_fusion.2
  49.4 1.9 fusion.40
  51.3 0.0 all-reduce.8.cloned.1.call-update
  51.3 0.0 all-reduce.10.cloned.1.call-start
  51.3 0.7 compare_select_fusion
  52.0 0.7 compare_and_fusion
  52.7 86.1 %all-reduce.8.cloned.1.call-done = f32[64,2,8,128]{3,2,1,0:T(8,128)} async-done(((f32[64,2,8,128]{3,2,1,0:T(8,128)}), f32[64,2,8,128]{3,2,1,0:T(8,128)}) %all-reduce.8.cloned.1.call-update) | async-done | bytes 524304 | tf_op jit(solution)/shard_map/psum | solution.py:91
  138.7 1.8 multiply_reduce_fusion.2
  140.5 5.5 %psum.79 = f32[]{:T(128)} all-reduce(f32[]{:T(128)} %multiply_reduce_fusion.2), channel_id=1, replica_groups=mesh['ray'=16,'vox'=2] {'vox'}, use_global_device_ids=true, to_apply=%region_5.7 | all-reduce | flops 1 | bytes 8 | tf_op jit(solution)/shard_map/psum | solution.py:76
  146.7 1.1 fusion.64
  147.9 0.1 fusion.67
  148.0 1.3 collective-permute-start
  149.3 4.5 %collective-permute-start.1 = (f32[64,2,1,128]{3,2,1,0:T(1,128)S(1)}, f32[64,2,1,128]{3,2,1,0:T(1,128)S(1)}, u32[]{:S(2)}, u32[]{:S(2)}) collective-permute-start(f32[64,2,1,128]{3,2,1,0:T(1,128)S(1)} %get-tuple-element.26), channel_id=1, source_target_pairs={{0,1},{2,3},{4,5},{6,7},{8,9},{10,11},{12,13},{14,15},{16,17},{18,... | collective-permute-start | bytes 196616 | tf_op jit(solution)/shard_map/ppermute | solution.py:23
  153.8 0.6 gather_fusion.1
  154.4 0.1 select_bitcast_fusion.2
  154.5 0.6 fusion.9
  155.1 0.2 convolution_bitcast_fusion.1
  155.3 0.4 collective-permute-done.1
  155.7 2.4 select_maximum_fusion.4
  158.1 0.0 copy-start.2
  158.1 1.5 multiply_reduce_fusion.1
  159.6 5.9 %all-reduce.4 = (f32[1024]{0:T(1024)S(1)}, f32[]{:T(128)}) all-reduce(f32[1024]{0:T(1024)S(1)} %convolution_bitcast_fusion.1, f32[]{:T(128)} %get-tuple-element.16), channel_id=1, replica_groups=mesh['ray'=16,'vox'=2] {'vox'}, use_global_device_ids=true, to_apply=%region_6.9 | all-reduce | flops 1025 | bytes 8200 | tf_op jit(solution)/shard_map/psum | solution.py:117
  165.6 0.6 multiply_reduce_fusion.4
  166.2 30.1 %psum.81 = f32[]{:T(128)} all-reduce(f32[]{:T(128)} %get-tuple-element.14), channel_id=1, replica_groups=mesh['ray'=16,'vox'=2] {'ray'}, use_global_device_ids=true, to_apply=%region_8.11 | all-reduce | flops 1 | bytes 8 | tf_op jit(solution)/shard_map/psum | solution.py:73
  197.6 0.1 broadcast_multiply_fusion
  197.8 0.1 fusion.66
  197.8 1.3 collective-permute-start.2
  199.1 4.5 %collective-permute-start.3 = (f32[64,2,1,128]{3,2,1,0:T(1,128)S(1)}, f32[64,2,1,128]{3,2,1,0:T(1,128)S(1)}, u32[]{:S(2)}, u32[]{:S(2)}) collective-permute-start(f32[64,2,1,128]{3,2,1,0:T(1,128)S(1)} %get-tuple-element.24), channel_id=1, source_target_pairs={{0,1},{2,3},{4,5},{6,7},{8,9},{10,11},{12,13},{14,15},{16,17},{18,... | collective-permute-start | bytes 196616 | tf_op jit(solution)/shard_map/ppermute | solution.py:23
  203.7 0.6 gather_fusion.2
  204.3 0.1 select_bitcast_fusion.1
  204.4 0.4 fusion.7
  204.8 1.2 fusion.39
  206.1 0.0 all-reduce.10.cloned.1.call-update
  206.2 3.7 %select_maximum_fusion.2 = f32[66,4,10,130]{3,2,1,0:T(8,128)} fusion(f32[64,2,1,128]{3,2,1,0:T(1,128)S(1)} %collective-permute-done.2, f32[64,2,8,128]{3,2,1,0:T(8,128)S(1)} %broadcast_multiply_fusion, f32[64,2,1,128]{3,2,1,0:T(1,128)S(1)} %collective-permute-done.3), kind=kLoop, calls=%fused_computation.12 | loop fusion | flops 7550400 | bytes 2028160 | tf_op jit(solution)/shard_map/concatenate | solution.py:27
  210.0 82.2 %all-reduce.10.cloned.1.call-done = f32[64,2,8,128]{3,2,1,0:T(8,128)} async-done(((f32[64,2,8,128]{3,2,1,0:T(8,128)}), f32[64,2,8,128]{3,2,1,0:T(8,128)}) %all-reduce.10.cloned.1.call-update) | async-done | bytes 524304 | tf_op jit(solution)/shard_map/psum | solution.py:91
  292.2 6.6 %multiply_reduce_fusion = (f32[]{:T(128)}, f32[64,2,8,128]{3,2,1,0:T(8,128)S(1)}) fusion(f32[64,2,8,128]{3,2,1,0:T(8,128)S(1)} %get-tuple-element.19, f32[]{:T(128)S(6)} %sqrt.23, f32[64,2,8,128]{3,2,1,0:T(8,128)} %all-reduce.10.cloned.1.call-done, f32[66,4,10,130]{3,2,1,0:T(8,128)} %select_maximum_fusion.2, ...), kind=kLoop, calls=%fused_computation.75 | loop fusion | flops 2359295 | bytes 5373960 | tf_op jit(solution)/shard_map/reduce_sum | solution.py:76
  298.9 5.5 %psum.84 = f32[]{:T(128)} all-reduce(f32[]{:T(128)} %get-tuple-element.12), channel_id=1, replica_groups=mesh['ray'=16,'vox'=2] {'vox'}, use_global_device_ids=true, to_apply=%region_13.16 | all-reduce | flops 1 | bytes 8 | tf_op jit(solution)/shard_map/psum | solution.py:76
  305.1 0.1 fusion.61
  305.2 0.1 fusion.65
  305.3 1.3 collective-permute-start.4
  306.6 4.5 %collective-permute-start.5 = (f32[64,2,1,128]{3,2,1,0:T(1,128)S(1)}, f32[64,2,1,128]{3,2,1,0:T(1,128)S(1)}, u32[]{:S(2)}, u32[]{:S(2)}) collective-permute-start(f32[64,2,1,128]{3,2,1,0:T(1,128)S(1)} %get-tuple-element.22), channel_id=1, source_target_pairs={{0,1},{2,3},{4,5},{6,7},{8,9},{10,11},{12,13},{14,15},{16,17},{18,... | collective-permute-start | bytes 196616 | tf_op jit(solution)/shard_map/ppermute | solution.py:23
  311.1 0.6 gather_fusion.3
  311.7 0.1 select_bitcast_fusion
  311.8 0.6 fusion.5
  312.5 0.2 convolution_bitcast_fusion
  312.7 0.3 collective-permute-done.5
  313.0 2.4 select_maximum_fusion
  315.4 1.6 fusion.18
  317.0 5.9 %all-reduce.3 = (f32[1024]{0:T(1024)S(1)}, f32[]{:T(128)}) all-reduce(f32[1024]{0:T(1024)S(1)} %convolution_bitcast_fusion, f32[]{:T(128)} %fusion.18), channel_id=1, replica_groups=mesh['ray'=16,'vox'=2] {'vox'}, use_global_device_ids=true, to_apply=%region_14.17 | all-reduce | flops 1025 | bytes 8200 | tf_op jit(solution)/shard_map/psum | solution.py:117
  322.9 0.6 multiply_reduce_fusion.3
  323.5 30.1 %psum.86 = f32[]{:T(128)} all-reduce(f32[]{:T(128)} %get-tuple-element.8), channel_id=1, replica_groups=mesh['ray'=16,'vox'=2] {'ray'}, use_global_device_ids=true, to_apply=%region_16.19 | all-reduce | flops 1 | bytes 8 | tf_op jit(solution)/shard_map/psum | solution.py:73
  355.0 0.6 broadcast_divide_fusion.3
  355.7 0.6 fusion.44
  (13 shorter events, 0.0 us)
Async XLA Ops:
  7.2 41.1 %copy-start = (bf16[1,1,32,128,128]{4,3,2,1,0:T(8,128)(2,1)S(1)}, bf16[1,1,32,128,128]{4,3,2,1,0:T(8,128)(2,1)}, u32[]{:S(2)}) copy-start(bf16[1,1,32,128,128]{4,3,2,1,0:T(8,128)(2,1)} %param.13) | copy-start | bytes 3145732
  7.2 148.0 %copy-start.3 = (s32[1,1,32]{2,1,0:T(1,128)S(1)}, s32[1,1,32]{2,1,0:T(1,128)}, u32[]{:S(2)}) copy-start(s32[1,1,32]{2,1,0:T(1,128)} %param.15) | copy-start | bytes 388
  7.2 131.5 %all-reduce.8.cloned.1.call-start = ((), (), s32[]{:S(2)}) async-start(), calls=%async_computation | async-start | bytes 1048576 | tf_op jit(solution)/shard_map/psum | solution.py:91
  51.3 106.8 %copy-start.1 = (f32[64]{0:T(128)S(1)}, f32[64]{0:T(128)}, u32[]{:S(2)}) copy-start(f32[64]{0:T(128)} %param.21) | copy-start | bytes 772
  51.3 240.9 %all-reduce.10.cloned.1.call-start = ((), (), s32[]{:S(2)}) async-start(), calls=%async_computation.1 | async-start | bytes 1048576 | tf_op jit(solution)/shard_map/psum | solution.py:91
  148.0 7.4 %collective-permute-start = (f32[64,2,1,128]{3,2,1,0:T(1,128)S(1)}, f32[64,2,1,128]{3,2,1,0:T(1,128)S(1)}, u32[]{:S(2)}, u32[]{:S(2)}) collective-permute-start(f32[64,2,1,128]{3,2,1,0:T(1,128)S(1)} %get-tuple-element.27), channel_id=1, source_target_pairs={{1,0},{3,2},{5,4},{7,6},{9,8},{11,10},{13,12},{15,14},{17,16},{19,... | collective-permute-start | bytes 196616 | tf_op jit(solution)/shard_map/ppermute | solution.py:26
  149.3 6.4 %collective-permute-start.1 = (f32[64,2,1,128]{3,2,1,0:T(1,128)S(1)}, f32[64,2,1,128]{3,2,1,0:T(1,128)S(1)}, u32[]{:S(2)}, u32[]{:S(2)}) collective-permute-start(f32[64,2,1,128]{3,2,1,0:T(1,128)S(1)} %get-tuple-element.26), channel_id=1, source_target_pairs={{0,1},{2,3},{4,5},{6,7},{8,9},{10,11},{12,13},{14,15},{16,17},{18,... | collective-permute-start | bytes 196616 | tf_op jit(solution)/shard_map/ppermute | solution.py:23
  158.1 46.7 %copy-start.2 = (s32[1,1,32]{2,1,0:T(1,128)S(1)}, s32[1,1,32]{2,1,0:T(1,128)}, u32[]{:S(2)}) copy-start(s32[1,1,32]{2,1,0:T(1,128)} %param.16) | copy-start | bytes 388
  197.8 8.4 %collective-permute-start.2 = (f32[64,2,1,128]{3,2,1,0:T(1,128)S(1)}, f32[64,2,1,128]{3,2,1,0:T(1,128)S(1)}, u32[]{:S(2)}, u32[]{:S(2)}) collective-permute-start(f32[64,2,1,128]{3,2,1,0:T(1,128)S(1)} %get-tuple-element.25), channel_id=1, source_target_pairs={{1,0},{3,2},{5,4},{7,6},{9,8},{11,10},{13,12},{15,14},{17,16},{19,... | collective-permute-start | bytes 196616 | tf_op jit(solution)/shard_map/ppermute | solution.py:26
  199.1 7.1 %collective-permute-start.3 = (f32[64,2,1,128]{3,2,1,0:T(1,128)S(1)}, f32[64,2,1,128]{3,2,1,0:T(1,128)S(1)}, u32[]{:S(2)}, u32[]{:S(2)}) collective-permute-start(f32[64,2,1,128]{3,2,1,0:T(1,128)S(1)} %get-tuple-element.24), channel_id=1, source_target_pairs={{0,1},{2,3},{4,5},{6,7},{8,9},{10,11},{12,13},{14,15},{16,17},{18,... | collective-permute-start | bytes 196616 | tf_op jit(solution)/shard_map/ppermute | solution.py:23
  305.3 7.4 %collective-permute-start.4 = (f32[64,2,1,128]{3,2,1,0:T(1,128)S(1)}, f32[64,2,1,128]{3,2,1,0:T(1,128)S(1)}, u32[]{:S(2)}, u32[]{:S(2)}) collective-permute-start(f32[64,2,1,128]{3,2,1,0:T(1,128)S(1)} %get-tuple-element.23), channel_id=1, source_target_pairs={{1,0},{3,2},{5,4},{7,6},{9,8},{11,10},{13,12},{15,14},{17,16},{19,... | collective-permute-start | bytes 196616 | tf_op jit(solution)/shard_map/ppermute | solution.py:26
  306.6 6.4 %collective-permute-start.5 = (f32[64,2,1,128]{3,2,1,0:T(1,128)S(1)}, f32[64,2,1,128]{3,2,1,0:T(1,128)S(1)}, u32[]{:S(2)}, u32[]{:S(2)}) collective-permute-start(f32[64,2,1,128]{3,2,1,0:T(1,128)S(1)} %get-tuple-element.22), channel_id=1, source_target_pairs={{0,1},{2,3},{4,5},{6,7},{8,9},{10,11},{12,13},{14,15},{16,17},{18,... | collective-permute-start | bytes 196616 | tf_op jit(solution)/shard_map/ppermute | solution.py:23
Sparse Core Ops, SparseCore 0:
  51.4 87.2 all-reduce.7
  206.3 85.8 all-reduce.9
where the time goes:
time: 364 us; the launch traced here: 363 us
  waiting for transfers between devices  169 us (46%)
  blocking collectives  119 us (33%)
  other arithmetic  29.7 us (8%)
  between operations  20 us (5%)
  starting transfers between devices  17.6 us (5%)
  matrix products  5.56 us (2%)
    psum x2, waiting for transfers between devices, pull_back(): return lax.psum(summed, 'ray')  168 us
    psum x3, blocking collectives, ray_total(): return lax.psum(jnp.sum(values * values), 'ray')  95.7 us
    ppermute x3, starting transfers between devices, with_halo(): lax.ppermute(lax.slice_in_dim(block, block.shape[dim] - width, None, axis...  13.6 us
    psum x2, blocking collectives, on_device(): ray_sums = lax.psum(partial_value, 'vox')  11.9 us
    reduce_sum x4, other arithmetic, slab_total(): return lax.psum(jnp.sum(values * values), 'vox')  11.6 us
    psum x2, blocking collectives, slab_total(): return lax.psum(jnp.sum(values * values), 'vox')  11.1 us
    concatenate x3, other arithmetic, with_halo(): block = jnp.concatenate([low, block, high], axis=dim)  8.48 us
  transfers between devices with their start and end apart: 8, of which 4 were waited for; matrix products, arithmetic and copies ran while one was open for 3% of the time, Pallas kernels for 0%

commit v1 on v0

--- a/solution.py
+++ b/solution.py
@@ -13,6 +13,11 @@
 LATERAL = 1.0
 VERTICAL = 4.0
 TEMPORAL = 0.5
+
+
+def gather_and_add(array, name):
+    parts = lax.all_gather(array, name)
+    return jnp.sum(parts, axis=0)
 
 
 def with_halo(block, sides, width):
@@ -88,7 +93,7 @@
         summed = jnp.dot(onehot, contrib, precision=lax.Precision.HIGHEST).reshape(
             ALT, EPOCHS, LON_DEV, LAT
         )
-        return lax.psum(summed, "ray")
+        return gather_and_add(summed, "ray")
 
     def right_norm_of(values):
         return jnp.sqrt(slab_total(values))

time: 364 us -> 339 us (0.931)
  waiting for transfers between devices: 169 us -> 137 us
  other arithmetic: 29.7 us -> 36.2 us
    psum x2 -> x0, waiting for transfers between devices: 168 us -> none  [pull_back(): return lax.psum(summed, 'ray')]
    all_gather x0 -> x2, waiting for transfers between devices: none -> 132 us  [gather_and_add(): parts = lax.all_gather(array, name)]
    reduce_sum x0 -> x2, other arithmetic: none -> 8.78 us  [gather_and_add(): return jnp.sum(parts, axis=0)]
    ppermute x3, waiting for transfers between devices: 0.68 us -> 4.74 us  [with_halo(): lax.ppermute(lax.slice_in_dim(block, block.shape[dim] - width, None, axis...]
  transfers between devices with their start and end apart: 8 -> 8, of which waited for: 4 -> 8; matrix products, arithmetic and copies ran while one was open for 3% -> 2% of each run, Pallas kernels for 0% -> 0%
where the time goes in v1:
time: 339 us; the launch traced here: 338 us
  waiting for transfers between devices  137 us (40%)
  blocking collectives  119 us (35%)
  other arithmetic  36.2 us (11%)
  between operations  20 us (6%)
  starting transfers between devices  17.6 us (5%)
  matrix products  5.6 us (2%)
    all_gather x2, waiting for transfers between devices, gather_and_add(): parts = lax.all_gather(array, name)  132 us
    psum x3, blocking collectives, ray_total(): return lax.psum(jnp.sum(values * values), 'ray')  95.7 us
    ppermute x3, starting transfers between devices, with_halo(): lax.ppermute(lax.slice_in_dim(block, block.shape[dim] - width, None, axis...  13.6 us
    psum x2, blocking collectives, on_device(): ray_sums = lax.psum(partial_value, 'vox')  11.9 us
    psum x2, blocking collectives, slab_total(): return lax.psum(jnp.sum(values * values), 'vox')  11.1 us
    reduce_sum x4, other arithmetic, slab_total(): return lax.psum(jnp.sum(values * values), 'vox')  10.4 us
    reduce_sum x2, other arithmetic, gather_and_add(): return jnp.sum(parts, axis=0)  8.78 us
    concatenate x3, other arithmetic, with_halo(): block = jnp.concatenate([low, block, high], axis=dim)  8.48 us
  transfers between devices with their start and end apart: 8, of which 8 were waited for; matrix products, arithmetic and copies ran while one was open for 2% of the time, Pallas kernels for 0%

profile of v1, /device:TPU:0, one launch (start us, length us, event | category | flops | bytes accessed | tf_op | source)
XLA Modules:
  0.0 338.0 jit_solution(16751635298707591207)
XLA Ops:
  7.2 0.7 compare_select_fusion.1
  8.0 0.7 compare_and_fusion.1
  8.6 0.8 select_reduce_fusion
  9.5 1.3 multiply_reduce_fusion.5
  10.7 35.5 %psum.63 = f32[]{:T(128)} all-reduce(f32[]{:T(128)} %get-tuple-element.20), channel_id=1, replica_groups=mesh['ray'=16,'vox'=2] {'ray'}, use_global_device_ids=true, to_apply=%region_2.3 | all-reduce | flops 1 | bytes 8 | tf_op jit(solution)/shard_map/psum | solution.py:78
  47.6 0.6 gather_fusion
  48.2 0.1 select_bitcast_fusion.3
  48.3 0.4 fusion.11
  48.7 0.7 compare_select_fusion.2
  49.3 1.9 fusion.40
  51.3 0.0 all-gather.5.cloned.1.call-start
  51.3 0.7 compare_select_fusion
  52.0 0.7 compare_and_fusion
  52.7 71.0 %all-gather.3.cloned.1.call-done = f32[16,64,2,8,128]{4,3,2,1,0:T(8,128)} async-done(((f32[1,64,2,8,128]{4,3,2,1,0:T(8,128)}), f32[16,64,2,8,128]{4,3,2,1,0:T(8,128)}) %all-gather.3.cloned.1.call-update) | async-done | bytes 8388624 | tf_op jit(solution)/shard_map/all_gather | solution.py:19
  123.6 4.0 %reduce_sum.92 = f32[64,2,8,128]{3,2,1,0:T(8,128)S(1)} reduce(f32[16,64,2,8,128]{4,3,2,1,0:T(8,128)} %all-gather.3.cloned.1.call-done, f32[]{:T(128)} %constant.25.clone.1), dimensions={0}, to_apply=%region_3.5 | reduce | flops 1966080 | bytes 8912900 | tf_op jit(solution)/shard_map/reduce_sum | solution.py:20
  127.6 0.7 multiply_reduce_fusion.2
  128.4 5.6 %psum.64 = f32[]{:T(128)} all-reduce(f32[]{:T(128)} %multiply_reduce_fusion.2), channel_id=1, replica_groups=mesh['ray'=16,'vox'=2] {'vox'}, use_global_device_ids=true, to_apply=%region_5.7 | all-reduce | flops 1 | bytes 8 | tf_op jit(solution)/shard_map/psum | solution.py:81
  134.6 0.1 fusion.64
  134.7 0.6 gather_fusion.1
  135.3 0.1 select_bitcast_fusion.2
  135.4 0.6 fusion.9
  136.0 0.1 fusion.67
  136.1 1.3 collective-permute-start
  137.4 4.5 %collective-permute-start.1 = (f32[64,2,1,128]{3,2,1,0:T(1,128)S(1)}, f32[64,2,1,128]{3,2,1,0:T(1,128)S(1)}, u32[]{:S(2)}, u32[]{:S(2)}) collective-permute-start(f32[64,2,1,128]{3,2,1,0:T(1,128)S(1)} %get-tuple-element.26), channel_id=1, source_target_pairs={{0,1},{2,3},{4,5},{6,7},{8,9},{10,11},{12,13},{14,15},{16,17},{18,... | collective-permute-start | bytes 196616 | tf_op jit(solution)/shard_map/ppermute | solution.py:28
  142.0 0.2 convolution_bitcast_fusion.1
  142.2 0.1 collective-permute-done
  142.3 1.6 collective-permute-done.1
  143.8 2.4 select_maximum_fusion.4
  146.2 1.5 multiply_reduce_fusion.1
  147.8 5.9 %all-reduce.4 = (f32[1024]{0:T(1024)S(1)}, f32[]{:T(128)}) all-reduce(f32[1024]{0:T(1024)S(1)} %convolution_bitcast_fusion.1, f32[]{:T(128)} %get-tuple-element.16), channel_id=1, replica_groups=mesh['ray'=16,'vox'=2] {'vox'}, use_global_device_ids=true, to_apply=%region_6.9 | all-reduce | flops 1025 | bytes 8200 | tf_op jit(solution)/shard_map/psum | solution.py:122
  153.7 0.6 multiply_reduce_fusion.4
  154.3 30.1 %psum.66 = f32[]{:T(128)} all-reduce(f32[]{:T(128)} %get-tuple-element.14), channel_id=1, replica_groups=mesh['ray'=16,'vox'=2] {'ray'}, use_global_device_ids=true, to_apply=%region_8.11 | all-reduce | flops 1 | bytes 8 | tf_op jit(solution)/shard_map/psum | solution.py:78
  185.7 0.6 gather_fusion.2
  186.3 0.1 select_bitcast_fusion.1
  186.4 0.4 fusion.7
  186.8 1.3 fusion.39
  188.1 0.1 broadcast_multiply_fusion
  188.2 0.1 fusion.66
  188.3 1.3 collective-permute-start.2
  189.6 4.5 %collective-permute-start.3 = (f32[64,2,1,128]{3,2,1,0:T(1,128)S(1)}, f32[64,2,1,128]{3,2,1,0:T(1,128)S(1)}, u32[]{:S(2)}, u32[]{:S(2)}) collective-permute-start(f32[64,2,1,128]{3,2,1,0:T(1,128)S(1)} %get-tuple-element.24), channel_id=1, source_target_pairs={{0,1},{2,3},{4,5},{6,7},{8,9},{10,11},{12,13},{14,15},{16,17},{18,... | collective-permute-start | bytes 196616 | tf_op jit(solution)/shard_map/ppermute | solution.py:28
  194.4 0.1 collective-permute-done.2
  194.5 1.6 collective-permute-done.3
  196.1 3.7 %select_maximum_fusion.2 = f32[66,4,10,130]{3,2,1,0:T(8,128)} fusion(f32[64,2,1,128]{3,2,1,0:T(1,128)S(1)} %collective-permute-done.2, f32[64,2,8,128]{3,2,1,0:T(8,128)S(1)} %broadcast_multiply_fusion, f32[64,2,1,128]{3,2,1,0:T(1,128)S(1)} %collective-permute-done.3), kind=kLoop, calls=%fused_computation.12 | loop fusion | flops 7550400 | bytes 2028160 | tf_op jit(solution)/shard_map/concatenate | solution.py:32
  199.8 61.2 %all-gather.5.cloned.1.call-done = f32[16,64,2,8,128]{4,3,2,1,0:T(8,128)} async-done(((f32[1,64,2,8,128]{4,3,2,1,0:T(8,128)}), f32[16,64,2,8,128]{4,3,2,1,0:T(8,128)}) %all-gather.5.cloned.1.call-update) | async-done | bytes 8388624 | tf_op jit(solution)/shard_map/all_gather | solution.py:19
  261.0 4.8 %reduce_sum.96 = f32[64,2,8,128]{3,2,1,0:T(8,128)} reduce(f32[16,64,2,8,128]{4,3,2,1,0:T(8,128)} %all-gather.5.cloned.1.call-done, f32[]{:T(128)} %constant.25.clone.1), dimensions={0}, to_apply=%region_11.14 | reduce | flops 1966080 | bytes 8912900 | tf_op jit(solution)/shard_map/reduce_sum | solution.py:20
  265.8 6.6 %multiply_reduce_fusion = (f32[]{:T(128)}, f32[64,2,8,128]{3,2,1,0:T(8,128)S(1)}) fusion(f32[64,2,8,128]{3,2,1,0:T(8,128)S(1)} %get-tuple-element.19, f32[]{:T(128)S(6)} %sqrt.23, f32[64,2,8,128]{3,2,1,0:T(8,128)} %reduce_sum.96, f32[66,4,10,130]{3,2,1,0:T(8,128)} %select_maximum_fusion.2, f32[64,2,8,128]{3,2,1,0:T(8,128)S(1)} %broadcast_multiply_fusion, ...), kind=kLoop, calls=%fused_computation.75 | loop fusion | flops 2359295 | bytes 5373960 | tf_op jit(solution)/shard_map/reduce_sum | solution.py:81
  272.3 5.5 %psum.68 = f32[]{:T(128)} all-reduce(f32[]{:T(128)} %get-tuple-element.12), channel_id=1, replica_groups=mesh['ray'=16,'vox'=2] {'vox'}, use_global_device_ids=true, to_apply=%region_13.16 | all-reduce | flops 1 | bytes 8 | tf_op jit(solution)/shard_map/psum | solution.py:81
  278.6 0.1 fusion.61
  278.6 0.6 gather_fusion.3
  279.2 0.1 select_bitcast_fusion
  279.3 0.6 fusion.5
  280.0 0.1 fusion.65
  280.1 1.3 collective-permute-start.4
  281.4 4.5 %collective-permute-start.5 = (f32[64,2,1,128]{3,2,1,0:T(1,128)S(1)}, f32[64,2,1,128]{3,2,1,0:T(1,128)S(1)}, u32[]{:S(2)}, u32[]{:S(2)}) collective-permute-start(f32[64,2,1,128]{3,2,1,0:T(1,128)S(1)} %get-tuple-element.22), channel_id=1, source_target_pairs={{0,1},{2,3},{4,5},{6,7},{8,9},{10,11},{12,13},{14,15},{16,17},{18,... | collective-permute-start | bytes 196616 | tf_op jit(solution)/shard_map/ppermute | solution.py:28
  286.0 0.2 convolution_bitcast_fusion
  286.2 0.1 collective-permute-done.4
  286.2 1.6 collective-permute-done.5
  287.8 2.4 select_maximum_fusion
  290.2 1.6 fusion.18
  291.8 5.9 %all-reduce.3 = (f32[1024]{0:T(1024)S(1)}, f32[]{:T(128)}) all-reduce(f32[1024]{0:T(1024)S(1)} %convolution_bitcast_fusion, f32[]{:T(128)} %fusion.18), channel_id=1, replica_groups=mesh['ray'=16,'vox'=2] {'vox'}, use_global_device_ids=true, to_apply=%region_14.17 | all-reduce | flops 1025 | bytes 8200 | tf_op jit(solution)/shard_map/psum | solution.py:122
  297.7 0.6 multiply_reduce_fusion.3
  298.3 30.1 %psum.70 = f32[]{:T(128)} all-reduce(f32[]{:T(128)} %get-tuple-element.8), channel_id=1, replica_groups=mesh['ray'=16,'vox'=2] {'ray'}, use_global_device_ids=true, to_apply=%region_16.19 | all-reduce | flops 1 | bytes 8 | tf_op jit(solution)/shard_map/psum | solution.py:78
  329.9 0.6 broadcast_divide_fusion.3
  330.5 0.6 fusion.44
  (15 shorter events, 0.1 us)
Async XLA Ops:
  7.2 41.1 %copy-start = (bf16[1,1,32,128,128]{4,3,2,1,0:T(8,128)(2,1)S(1)}, bf16[1,1,32,128,128]{4,3,2,1,0:T(8,128)(2,1)}, u32[]{:S(2)}) copy-start(bf16[1,1,32,128,128]{4,3,2,1,0:T(8,128)(2,1)} %param.13) | copy-start | bytes 3145732
  7.2 116.5 %all-gather.3.cloned.1.call-start = ((), (), s32[]{:S(2)}) async-start(), calls=%async_computation | async-start | bytes 8912896 | tf_op jit(solution)/shard_map/all_gather | solution.py:19
  51.3 209.7 %all-gather.5.cloned.1.call-start = ((), (), s32[]{:S(2)}) async-start(), calls=%async_computation.1 | async-start | bytes 8912896 | tf_op jit(solution)/shard_map/all_gather | solution.py:19
  52.7 89.3 %copy-start.3 = (s32[1,1,32]{2,1,0:T(1,128)S(1)}, s32[1,1,32]{2,1,0:T(1,128)}, u32[]{:S(2)}) copy-start(s32[1,1,32]{2,1,0:T(1,128)} %param.15) | copy-start | bytes 388
  127.6 18.6 %copy-start.1 = (f32[64]{0:T(128)S(1)}, f32[64]{0:T(128)}, u32[]{:S(2)}) copy-start(f32[64]{0:T(128)} %param.21) | copy-start | bytes 772
  136.1 6.2 %collective-permute-start = (f32[64,2,1,128]{3,2,1,0:T(1,128)S(1)}, f32[64,2,1,128]{3,2,1,0:T(1,128)S(1)}, u32[]{:S(2)}, u32[]{:S(2)}) collective-permute-start(f32[64,2,1,128]{3,2,1,0:T(1,128)S(1)} %get-tuple-element.27), channel_id=1, source_target_pairs={{1,0},{3,2},{5,4},{7,6},{9,8},{11,10},{13,12},{15,14},{17,16},{19,... | collective-permute-start | bytes 196616 | tf_op jit(solution)/shard_map/ppermute | solution.py:31
  137.4 6.4 %collective-permute-start.1 = (f32[64,2,1,128]{3,2,1,0:T(1,128)S(1)}, f32[64,2,1,128]{3,2,1,0:T(1,128)S(1)}, u32[]{:S(2)}, u32[]{:S(2)}) collective-permute-start(f32[64,2,1,128]{3,2,1,0:T(1,128)S(1)} %get-tuple-element.26), channel_id=1, source_target_pairs={{0,1},{2,3},{4,5},{6,7},{8,9},{10,11},{12,13},{14,15},{16,17},{18,... | collective-permute-start | bytes 196616 | tf_op jit(solution)/shard_map/ppermute | solution.py:28
  142.2 44.6 %copy-start.2 = (s32[1,1,32]{2,1,0:T(1,128)S(1)}, s32[1,1,32]{2,1,0:T(1,128)}, u32[]{:S(2)}) copy-start(s32[1,1,32]{2,1,0:T(1,128)} %param.16) | copy-start | bytes 388
  188.3 6.2 %collective-permute-start.2 = (f32[64,2,1,128]{3,2,1,0:T(1,128)S(1)}, f32[64,2,1,128]{3,2,1,0:T(1,128)S(1)}, u32[]{:S(2)}, u32[]{:S(2)}) collective-permute-start(f32[64,2,1,128]{3,2,1,0:T(1,128)S(1)} %get-tuple-element.25), channel_id=1, source_target_pairs={{1,0},{3,2},{5,4},{7,6},{9,8},{11,10},{13,12},{15,14},{17,16},{19,... | collective-permute-start | bytes 196616 | tf_op jit(solution)/shard_map/ppermute | solution.py:31
  189.6 6.4 %collective-permute-start.3 = (f32[64,2,1,128]{3,2,1,0:T(1,128)S(1)}, f32[64,2,1,128]{3,2,1,0:T(1,128)S(1)}, u32[]{:S(2)}, u32[]{:S(2)}) collective-permute-start(f32[64,2,1,128]{3,2,1,0:T(1,128)S(1)} %get-tuple-element.24), channel_id=1, source_target_pairs={{0,1},{2,3},{4,5},{6,7},{8,9},{10,11},{12,13},{14,15},{16,17},{18,... | collective-permute-start | bytes 196616 | tf_op jit(solution)/shard_map/ppermute | solution.py:28
  280.1 6.2 %collective-permute-start.4 = (f32[64,2,1,128]{3,2,1,0:T(1,128)S(1)}, f32[64,2,1,128]{3,2,1,0:T(1,128)S(1)}, u32[]{:S(2)}, u32[]{:S(2)}) collective-permute-start(f32[64,2,1,128]{3,2,1,0:T(1,128)S(1)} %get-tuple-element.23), channel_id=1, source_target_pairs={{1,0},{3,2},{5,4},{7,6},{9,8},{11,10},{13,12},{15,14},{17,16},{19,... | collective-permute-start | bytes 196616 | tf_op jit(solution)/shard_map/ppermute | solution.py:31
  281.4 6.4 %collective-permute-start.5 = (f32[64,2,1,128]{3,2,1,0:T(1,128)S(1)}, f32[64,2,1,128]{3,2,1,0:T(1,128)S(1)}, u32[]{:S(2)}, u32[]{:S(2)}) collective-permute-start(f32[64,2,1,128]{3,2,1,0:T(1,128)S(1)} %get-tuple-element.22), channel_id=1, source_target_pairs={{0,1},{2,3},{4,5},{6,7},{8,9},{10,11},{12,13},{14,15},{16,17},{18,... | collective-permute-start | bytes 196616 | tf_op jit(solution)/shard_map/ppermute | solution.py:28
Sparse Core Ops, SparseCore 0:
  51.4 72.1 all-gather.2
  188.2 72.6 all-gather.4
